TPU v7x, 256 devices: a whole 4x4x8 slice. The times are simulated.
256 devices in a mesh: seq: 64 (over x, z, core), head: 4 (over y).
Axes of the slice: x: 4, y: 4, z: 8, core: 2. Of those that a mesh axis runs over, the one named last changes fastest.
Arguments:
- face_rows: bfloat16 [16384, 1024], P('seq', 'head'), may hold values from -400 to 400
- norm_gain: float32 [1024], replicated, may hold values from 0.25 to 1.75
- w_qkv: bfloat16 [1024, 3, 1024], P(None, None, 'head'), may hold values from -1.875 to 1.875
- w_out: bfloat16 [1024, 1024], P('head'), may hold values from -0.1875 to 0.1875
- segments: int32 [16384], P('seq'), may hold values from 0 to 3, never falling along the last dimension, each value on 1 to 8192 neighbouring positions
Outputs:
- mixed: bfloat16 [16384, 1024], P('seq', 'head')
All inputs are finite; a program needn't handle non-finite values.
Results may differ from a plain program's by a relative error of at most 0.004.
The roundings to bfloat16 on the way count: a program that leaves them out, or rounds other values in their place, can miss the bound.
Values may be sent and summed in bfloat16 or wider, within the bound.
A program may use at most 128 MiB of HBM per device.

v0:
```python
import functools
import math
import jax
import jax.numpy as jnp
from jax import lax
from jax.sharding import PartitionSpec as P

HD = 128
epsilon = 1e-05
masked_score = -1e30


def attend_piece(states, piece, start, groups, head_count):
    keys_vals, key_segments = piece
    key_count = keys_vals.shape[1]
    head_size = keys_vals.shape[2] // head_count
    key_rows = keys_vals[0].reshape(key_count, head_count, head_size)
    value_rows = keys_vals[1].reshape(key_count, head_count, head_size)
    key_positions = lax.iota(jnp.int32, key_count)
    key_seg = key_segments[0].astype(jnp.float32)
    updated = []
    for group, state in zip(groups, states):
        group_queries, query_positions, query_seg = group

        def update(
            current,
            group_queries=group_queries,
            query_positions=query_positions,
            query_seg=query_seg,
        ):
            run_max, run_total, run_acc = current
            scores = jnp.einsum(
                "qhd,khd->hqk", group_queries, key_rows, preferred_element_type=jnp.float32
            )
            allowed = (key_positions[None, :] <= query_positions[:, None]) & (
                key_seg[None, :] == query_seg[:, None]
            )
            scores = jnp.where(allowed[None], scores, masked_score)
            new_max = jnp.maximum(run_max, jnp.max(scores, axis=2))
            factor = jnp.exp(run_max - new_max)
            weights = jnp.where(allowed[None], jnp.exp(scores - new_max[:, :, None]), 0.0)
            new_total = jnp.sum(weights, axis=2)
            new_acc = jnp.einsum(
                "hqk,khd->hqd",
                weights.astype(jnp.bfloat16),
                value_rows,
                preferred_element_type=jnp.float32,
            )
            return (new_max, new_total, new_acc)

        needed = (start <= jnp.max(query_positions)) & (
            key_seg[key_count - 1] >= jnp.min(query_seg)
        )
        updated.append(lax.cond(needed, update, lambda current: current, state))
    return tuple(updated)


def finish(state, width):
    run_max, run_total, run_acc = state
    result = run_acc / run_total[:, :, None]
    return jnp.transpose(result, (1, 0, 2)).reshape(result.shape[1], width).astype(jnp.bfloat16)


def per_device(face_rows, norm_gain, w_qkv, w_out, segments):
    whole = lax.all_gather(face_rows, "head", axis=1, tiled=True)
    row_count, model_width = whole.shape
    width = w_qkv.shape[2]
    head_count = width // HD
    half = row_count // 2
    values32 = whole.astype(jnp.float32)
    normed = (
        values32
        * lax.rsqrt(jnp.mean(values32 * values32, axis=1, keepdims=True) + epsilon)
        * norm_gain
    ).astype(jnp.bfloat16)
    projected = jnp.dot(
        normed, w_qkv.reshape(model_width, 3 * width), preferred_element_type=jnp.float32
    )
    queries = (projected[:, :width] * (1.0 / math.sqrt(HD))).astype(jnp.bfloat16)
    keys_vals = jnp.stack([projected[:, width : 2 * width], projected[:, 2 * width :]]).astype(
        jnp.bfloat16
    )
    shard_index = lax.axis_index("seq")
    positions = shard_index * row_count + lax.iota(jnp.int32, row_count)
    seg_values = segments.astype(jnp.float32)
    seg_wire = seg_values.astype(jnp.bfloat16)[None, :]
    lower = (queries[:half].reshape(half, head_count, HD), positions[:half], seg_values[:half])
    upper = (queries[half:].reshape(half, head_count, HD), positions[half:], seg_values[half:])
    groups = (lower, upper)
    start_state = (
        jnp.full((head_count, half), masked_score, jnp.float32),
        jnp.zeros((head_count, half), jnp.float32),
        jnp.zeros((head_count, half, HD), jnp.float32),
    )
    attend = functools.partial(attend_piece, groups=groups, head_count=head_count)
    states = attend(
        (start_state, start_state),
        (
            lax.all_gather(keys_vals, "seq", axis=1, tiled=True),
            lax.all_gather(seg_wire, "seq", axis=1, tiled=True),
        ),
        jnp.int32(0),
    )
    lower_out = finish(states[0], width)
    upper_out = finish(states[1], width)
    attended = jnp.concatenate([lower_out, upper_out], axis=0)
    partial_sums = jnp.dot(attended, w_out, preferred_element_type=jnp.float32)
    return lax.psum_scatter(partial_sums, "head", scatter_dimension=1, tiled=True).astype(
        jnp.bfloat16
    )


def solution(mesh):
    in_specs = (P("seq", "head"), P(), P(None, None, "head"), P("head", None), P("seq"))
    out_specs = P("seq", "head")
    return jax.shard_map(
        per_device, mesh=mesh, in_specs=in_specs, out_specs=out_specs, check_vma=False
    )
```

profile of v0, /device:TPU:2, one launch (start us, length us, event | category | flops | bytes accessed | tf_op | source)
XLA Modules:
  0.0 261.9 jit_solution(16025028984586071454)
XLA Ops:
  6.5 13.6 %all_gather.10 = bf16[256,1024]{1,0:T(8,128)(2,1)S(1)} all-gather(bf16[256,256]{1,0:T(8,128)(2,1)} %param.9), channel_id=1, replica_groups=mesh['seq'=64,'head'=4] {'head'}, dimensions={1}, use_global_device_ids=true | all-gather | bytes 655360 | tf_op jit(solution)/shard_map/all_gather | solution.py:65
  20.2 0.2 fusion.20
  20.4 1.7 copy.23
  22.1 1.3 fusion.37
  23.4 0.7 pad_maximum_fusion
  24.2 0.0 all-gather.4.cloned.1.call-update
  24.2 0.0 reduce-scatter.2.cloned.1.call-start
  24.3 46.5 %all-gather.1 = bf16[64,1,256]{2,1,0:T(2,128)(2,1)S(1)} all-gather(bf16[1,1,256]{2,1,0:T(2,128)(2,1)S(1)} %reshape.149), channel_id=2, replica_groups=mesh['seq'=64,'head'=4] {'seq'}, dimensions={0}, use_global_device_ids=true | all-gather | bytes 33280 | tf_op jit(solution)/shard_map/all_gather | solution.py:100
  70.8 0.1 convert_element_type.72
  70.9 0.7 slice.54
  71.5 0.7 slice_reduce_fusion.2
  73.6 0.7 slice_reduce_fusion.3
  76.9 48.2 %all-gather.4.cloned.1.call-done = bf16[2,16384,256]{2,1,0:T(8,128)(2,1)} async-done(((bf16[2,256,256]{2,1,0:T(8,128)(2,1)}), bf16[2,16384,256]{2,1,0:T(8,128)(2,1)}) %all-gather.4.cloned.1.call-update) | async-done | bytes 16777232 | tf_op jit(solution)/shard_map/all_gather | solution.py:99
  125.2 11.3 %fusion.35 = (bf16[1,16384,256]{2,1,0:T(8,128)(2,1)}, bf16[1,16384,256]{2,1,0:T(8,128)(2,1)}) fusion(bf16[2,16384,256]{2,1,0:T(8,128)(2,1)} %all-gather.4.cloned.1.call-done), kind=kLoop, calls=%fused_computation.55 | loop fusion | bytes 33554432 | tf_op jit(solution)/shard_map/slice | solution.py:18
  136.5 12.5 %reshape_squeeze.6 = bf16[16384,2,128]{2,1,0:T(2,128)(2,1)} reshape(bf16[1,16384,256]{2,1,0:T(8,128)(2,1)} %get-tuple-element.112) | data formatting | bytes 16777216 | tf_op jit(solution)/shard_map/reshape;squeeze | solution.py:17
  149.0 12.6 %reshape_squeeze.7 = bf16[16384,2,128]{2,1,0:T(2,128)(2,1)} reshape(bf16[1,16384,256]{2,1,0:T(8,128)(2,1)} %get-tuple-element.111) | data formatting | bytes 16777216 | tf_op jit(solution)/shard_map/reshape;squeeze | solution.py:18
  161.6 33.0 %conditional.2 = (f32[2,128]{1,0:T(2,128)S(1)}, f32[2,128,128]{1,2,0:T(8,128)S(1)}) conditional(s32[]{:T(128)} %convert_element_type.58, () %tuple.21, (s32[16384]{0:T(1024)S(1)}, s32[128]{0:T(128)S(1)}, f32[16384]{0:T(1024)S(1)}, f32[128]{0:T(128)S(1)}, bf16[256,256]{1,0:T(8,128)(2,1)S(1)}, /*index=5*/bf16[16384,2,128]{2,1,0:T(2,128)(2,1)}, ...), branch_computations={%region_3.0_spmd, %region_4.7_spmd} | conditional | flops 2187329280 | bytes 76487728 | solution.py:54
  161.6 0.6 copy-done.2
  162.2 2.5 compare_and_fusion
  164.7 0.1 copy.24
  164.9 10.7 %fusion.33 = (f32[2,128]{1,0:T(2,128)S(1)}, f32[2,128,16384]{2,1,0:T(8,128)}) fusion(bf16[128,2,128]{0,2,1:T(8,128)(2,1)S(1)} %bitcast.24, bf16[16384,2,128]{2,1,0:T(2,128)(2,1)} %get-tuple-element.92, pred[128,16384]{1,0:T(8,128)(4,1)S(1)} %compare_and_fusion), kind=kOutput, calls=%fused_computation.53 | convolution fusion | flops 1082130176 | bytes 27329536 | tf_op jit(solution)/shard_map/cond/branch_1_fun/qhd,khd->hqk/dot_general | solution.py:32
  175.5 11.1 %fusion.2 = f32[2,128,128]{1,2,0:T(8,128)S(1)} fusion(f32[2,128,16384]{2,1,0:T(8,128)} %get-tuple-element.108, bf16[16384,2,128]{2,1,0:T(2,128)(2,1)} %get-tuple-element.93, f32[2,128]{1,0:T(2,128)S(1)} %broadcast_maximum_fusion, pred[128,16384]{1,0:T(8,128)(4,1)S(1)} %compare_and_fusion), kind=kOutput, calls=%fused_computation.4 | convolution fusion | flops 1086324736 | bytes 27395072 | tf_op jit(solution)/shard_map/cond | solution.py:54
  186.6 8.0 %fusion.1 = f32[2,128]{1,0:T(2,128)S(1)} fusion(f32[2,128,16384]{2,1,0:T(8,128)} %get-tuple-element.108, f32[2,128]{1,0:T(2,128)S(1)} %broadcast_maximum_fusion, pred[128,16384]{1,0:T(8,128)(4,1)S(1)} %compare_and_fusion), kind=kLoop, calls=%fused_computation.3 | loop fusion | flops 12582656 | bytes 18876416 | tf_op jit(solution)/shard_map/cond/branch_1_fun/reduce_sum | solution.py:42
  194.7 32.6 %conditional.3 = (f32[2,128]{1,0:T(2,128)S(1)}, f32[2,128,128]{1,2,0:T(8,128)S(1)}) conditional(s32[]{:T(128)} %convert_element_type.66, () %tuple.23, (s32[16384]{0:T(1024)S(1)}, s32[128]{0:T(128)S(1)}, f32[16384]{0:T(1024)}, f32[128]{0:T(128)S(1)}, bf16[256,256]{1,0:T(8,128)(2,1)S(1)}, /*index=5*/bf16[16384,2,128]{2,1,0:T(2,128)(2,1)}, ...), branch_computations={%region_9.10_spmd, %region_10.13_spmd} | conditional | flops 2187329280 | bytes 76225552 | solution.py:54
  194.9 2.5 compare_and_fusion.1
  197.4 0.1 copy.28
  197.5 10.7 %fusion.34 = (f32[2,128]{1,0:T(2,128)S(1)}, f32[2,128,16384]{2,1,0:T(8,128)}) fusion(bf16[128,2,128]{0,2,1:T(8,128)(2,1)S(1)} %bitcast.25, bf16[16384,2,128]{2,1,0:T(2,128)(2,1)} %get-tuple-element.99, pred[128,16384]{1,0:T(8,128)(4,1)S(1)} %compare_and_fusion.1), kind=kOutput, calls=%fused_computation.54 | convolution fusion | flops 1082130176 | bytes 27329536 | tf_op jit(solution)/shard_map/cond/branch_1_fun/qhd,khd->hqk/dot_general | solution.py:32
  208.2 11.1 %fusion.12 = f32[2,128,128]{1,2,0:T(8,128)S(1)} fusion(f32[2,128,16384]{2,1,0:T(8,128)} %get-tuple-element.110, bf16[16384,2,128]{2,1,0:T(2,128)(2,1)} %get-tuple-element.100, f32[2,128]{1,0:T(2,128)S(1)} %broadcast_maximum_fusion.1, pred[128,16384]{1,0:T(8,128)(4,1)S(1)} %compare_and_fusion.1), kind=kOutput, calls=%fused_computation.17 | convolution fusion | flops 1086324736 | bytes 27395072 | tf_op jit(solution)/shard_map/cond | solution.py:54
  219.2 8.0 %fusion.11 = f32[2,128]{1,0:T(2,128)S(1)} fusion(f32[2,128,16384]{2,1,0:T(8,128)} %get-tuple-element.110, f32[2,128]{1,0:T(2,128)S(1)} %broadcast_maximum_fusion.1, pred[128,16384]{1,0:T(8,128)(4,1)S(1)} %compare_and_fusion.1), kind=kLoop, calls=%fused_computation.16 | loop fusion | flops 12582656 | bytes 18876416 | tf_op jit(solution)/shard_map/cond/branch_1_fun/reduce_sum | solution.py:42
  227.3 1.3 fusion.28
  228.6 24.8 %reduce-scatter.2.cloned.1.call-done = f32[256,256]{1,0:T(8,128)} async-done(((f32[256,1024]{1,0:T(8,128)}), f32[256,256]{1,0:T(8,128)}) %reduce-scatter.2.cloned.1.call-update) | async-done | bytes 262160 | tf_op jit(solution)/shard_map/reduce_scatter | solution.py:108
  253.4 1.6 convert_element_type.70
  (23 shorter events, 0.2 us)
Async XLA Ops:
  6.5 220.8 %copy-start = (bf16[256,1024]{1,0:T(8,128)(2,1)S(1)}, bf16[256,1024]{1,0:T(8,128)(2,1)}, u32[]{:S(2)}) copy-start(bf16[256,1024]{1,0:T(8,128)(2,1)} %param.12) | copy-start | bytes 1572868
  6.5 17.7 %copy-start.3 = (s32[256]{0:T(256)S(1)}, s32[256]{0:T(256)}, u32[]{:S(2)}) copy-start(s32[256]{0:T(256)} %param.13) | copy-start | bytes 3076
  6.5 118.6 %all-gather.4.cloned.1.call-start = ((), (), s32[]{:S(2)}) async-start(), calls=%async_computation.1 | async-start | bytes 17039360 | tf_op jit(solution)/shard_map/all_gather | solution.py:99
  24.2 229.2 %reduce-scatter.2.cloned.1.call-start = ((), (), s32[]{:S(2)}) async-start(), calls=%async_computation.2 | async-start | bytes 1310720 | tf_op jit(solution)/shard_map/reduce_scatter | solution.py:108
  70.8 90.7 %copy-start.1 = (f32[64,1,256]{2,1,0:T(1,128)}, f32[64,1,256]{2,1,0:T(1,128)S(1)}, u32[]{:S(2)}) copy-start(f32[64,1,256]{2,1,0:T(1,128)S(1)} %convert_element_type.72) | copy-start | bytes 196612
  161.6 0.6 copy-start.2
Sparse Core Ops, SparseCore 0:
  24.3 100.7 all-gather.3
  228.8 24.6 reduce-scatter.1
where the time goes:
time: 263 us; the launch traced here: 262 us
  waiting for transfers between devices  73 us (28%)
  blocking collectives  60.1 us (23%)
  matrix products  46 us (17%)
  local copies, waits for them, and re-layouts  39.6 us (15%)
  other arithmetic  25.2 us (10%)
  between operations  17.5 us (7%)
    all_gather x1, waiting for transfers between devices, per_device(): lax.all_gather(keys_vals, 'seq', axis=1, tiled=True)  48.2 us
    all_gather x1, blocking collectives, per_device(): lax.all_gather(seg_wire, 'seq', axis=1, tiled=True)  46.5 us
    reduce_scatter x1, waiting for transfers between devices, per_device(): lax.psum_scatter(partial_sums, 'head', scatter_dimension=1, tiled=True)  24.8 us
    cond x2, matrix products, attend_piece(): updated.append(lax.cond(needed, update, lambda current: current, state))  22.1 us
    dot_general x2, matrix products, update(): jnp.einsum('qhd,khd->hqk', group_queries, key_rows, preferred_element_typ...  21.3 us
    reduce_sum x2, other arithmetic, update(): new_total = jnp.sum(weights, axis=2)  16 us
    all_gather x1, blocking collectives, per_device(): whole = lax.all_gather(face_rows, 'head', axis=1, tiled=True)  13.6 us
    another operation x1, local copies, waits for them, and re-layouts, attend_piece(): value_rows = keys_vals[1].reshape(key_count, head_count, head_size)  12.6 us
  transfers between devices with their start and end apart: 2, of which 2 were waited for; matrix products, arithmetic and copies ran while one was open for 1% of the time, Pallas kernels for 0%

commit v1 on v0

--- a/solution.py
+++ b/solution.py
@@ -96,7 +96,9 @@
     states = attend(
         (start_state, start_state),
         (
-            lax.all_gather(keys_vals, "seq", axis=1, tiled=True),
+            jnp.concatenate(
+                lax.all_to_all(jnp.stack([keys_vals] * lax.axis_size("seq")), "seq", 0, 0), axis=1
+            ),
             lax.all_gather(seg_wire, "seq", axis=1, tiled=True),
         ),
         jnp.int32(0),

time: 263 us -> 612 us (2.33)
  blocking collectives: 60.1 us -> 412 us
  waiting for transfers between devices: 73 us -> 25.2 us
  local copies, waits for them, and re-layouts: 39.6 us -> 70.6 us
  starting transfers between devices: 0.04 us -> 12.4 us
    all_gather x1, blocking collectives: 46.5 us -> 398 us  [per_device(): lax.all_gather(seg_wire, 'seq', axis=1, tiled=True)]
    all_gather x1 -> x0, waiting for transfers between devices: 48.2 us -> none  [per_device(): lax.all_gather(keys_vals, 'seq', axis=1, tiled=True)]
    all_to_all x0 -> x1, starting transfers between devices: none -> 12.3 us  [per_device(): lax.all_to_all(jnp.stack([keys_vals] * lax.axis_size('seq')), 'seq', 0, 0)]
    slice x1 -> x2, local copies, waits for them, and re-layouts: 11.3 us -> 23 us  [attend_piece(): value_rows = keys_vals[1].reshape(key_count, head_count, head_size)]
    slice x0 -> x1, local copies, waits for them, and re-layouts: none -> 11.4 us  [attend_piece(): key_rows = keys_vals[0].reshape(key_count, head_count, head_size)]
  transfers between devices with their start and end apart: 2 -> 2, of which waited for: 2 -> 1; matrix products, arithmetic and copies ran while one was open for 1% -> 0% of each run, Pallas kernels for 0% -> 0%
where the time goes in v1:
time: 612 us; the launch traced here: 611 us
  blocking collectives  412 us (67%)
  local copies, waits for them, and re-layouts  70.6 us (12%)
  matrix products  48.6 us (8%)
  waiting for transfers between devices  25.2 us (4%)
  other arithmetic  24.5 us (4%)
  between operations  17.5 us (3%)
  starting transfers between devices  12.4 us (2%)
    all_gather x1, blocking collectives, per_device(): lax.all_gather(seg_wire, 'seq', axis=1, tiled=True)  398 us
    reduce_scatter x1, waiting for transfers between devices, per_device(): lax.psum_scatter(partial_sums, 'head', scatter_dimension=1, tiled=True)  25.1 us
    dot_general x2, matrix products, update(): jnp.einsum('qhd,khd->hqk', group_queries, key_rows, preferred_element_typ...  25 us
    slice x2, local copies, waits for them, and re-layouts, attend_piece(): value_rows = keys_vals[1].reshape(key_count, head_count, head_size)  23 us
    cond x2, matrix products, attend_piece(): updated.append(lax.cond(needed, update, lambda current: current, state))  21 us
    reduce_sum x2, other arithmetic, update(): new_total = jnp.sum(weights, axis=2)  16 us
    all_gather x1, blocking collectives, per_device(): whole = lax.all_gather(face_rows, 'head', axis=1, tiled=True)  13.6 us
    another operation x1, local copies, waits for them, and re-layouts, attend_piece(): value_rows = keys_vals[1].reshape(key_count, head_count, head_size)  13.5 us
  transfers between devices with their start and end apart: 2, of which 1 were waited for; matrix products, arithmetic and copies ran while one was open for 0% of the time, Pallas kernels for 0%

profile of v1, /device:TPU:2, one launch (start us, length us, event | category | flops | bytes accessed | tf_op | source)
XLA Modules:
  0.0 611.1 jit_solution(3723414596709580286)
XLA Ops:
  6.5 13.6 %all_gather.7 = bf16[256,1024]{1,0:T(8,128)(2,1)S(1)} all-gather(bf16[256,256]{1,0:T(8,128)(2,1)} %param.9), channel_id=1, replica_groups=mesh['seq'=64,'head'=4] {'head'}, dimensions={1}, use_global_device_ids=true | all-gather | bytes 655360 | tf_op jit(solution)/shard_map/all_gather | solution.py:65
  20.2 0.2 fusion.16
  20.4 1.7 copy.20
  22.1 1.3 fusion.33
  23.5 0.1 copy.21
  23.6 6.0 stack.11
  29.6 12.3 %all-to-all-start = ((bf16[64,2,256,256]{2,3,1,0:T(8,128)(2,1)}), bf16[64,2,256,256]{2,3,1,0:T(8,128)(2,1)}, u32[]{:S(2)}, u32[]{:S(2)}) async-start(bf16[64,2,256,256]{2,3,1,0:T(8,128)(2,1)} %stack.11), calls=%async_computation | async-start | bytes 33554432 | tf_op jit(solution)/shard_map/all_to_all | solution.py:100
  42.0 398.2 %all-gather.1 = bf16[64,1,256]{2,1,0:T(2,128)(2,1)S(1)} all-gather(bf16[1,1,256]{2,1,0:T(2,128)(2,1)S(1)} %reshape.169), channel_id=2, replica_groups=mesh['seq'=64,'head'=4] {'seq'}, dimensions={0}, use_global_device_ids=true | all-gather | bytes 33280 | tf_op jit(solution)/shard_map/all_gather | solution.py:102
  440.3 0.6 slice.56
  440.9 0.7 slice_reduce_fusion.2
  442.9 0.7 slice_reduce_fusion.3
  446.3 11.6 %fusion.31 = (bf16[1,64,256,256]{2,3,0,1:T(8,128)(2,1)}, bf16[1,64,256,256]{2,3,0,1:T(8,128)(2,1)}) fusion(bf16[2,64,256,256]{2,3,0,1:T(8,128)(2,1)} %bitcast.8), kind=kLoop, calls=%fused_computation.51 | loop fusion | bytes 33554432 | tf_op jit(solution)/shard_map/slice | solution.py:18
  457.9 11.4 %copy.22 = bf16[1,64,256,256]{2,1,3,0:T(8,128)(2,1)} copy(bf16[1,64,256,256]{2,3,0,1:T(8,128)(2,1)} %get-tuple-element.98) | data formatting | bytes 16777216 | tf_op jit(solution)/shard_map/slice | solution.py:17
  469.3 13.5 %reshape_squeeze.6 = bf16[16384,2,128]{0,2,1:T(8,128)(2,1)} reshape(bf16[1,64,256,256]{2,1,3,0:T(8,128)(2,1)} %copy.22) | data formatting | bytes 16777216 | tf_op jit(solution)/shard_map/reshape;squeeze | solution.py:17
  482.7 11.4 %copy.23 = bf16[1,64,256,256]{2,1,3,0:T(8,128)(2,1)} copy(bf16[1,64,256,256]{2,3,0,1:T(8,128)(2,1)} %get-tuple-element.97) | data formatting | bytes 16777216 | tf_op jit(solution)/shard_map/slice | solution.py:18
  494.1 13.5 %reshape_squeeze.7 = bf16[16384,2,128]{0,2,1:T(8,128)(2,1)} reshape(bf16[1,64,256,256]{2,1,3,0:T(8,128)(2,1)} %copy.23) | data formatting | bytes 16777216 | tf_op jit(solution)/shard_map/reshape;squeeze | solution.py:18
  507.6 34.5 %conditional.2 = (f32[2,128]{1,0:T(2,128)S(1)}, f32[2,128,128]{1,2,0:T(8,128)S(1)}) conditional(s32[]{:T(128)} %convert_element_type.60, () %tuple.21, (s32[16384]{0:T(1024)S(1)}, s32[128]{0:T(128)S(1)}, f32[16384]{0:T(1024)S(1)}, f32[128]{0:T(128)S(1)}, bf16[256,256]{1,0:T(8,128)(2,1)S(1)}, /*index=5*/bf16[16384,2,128]{0,2,1:T(8,128)(2,1)}, ...), branch_computations={%region_3.0_spmd, %region_4.7_spmd} | conditional | flops 2187329280 | bytes 76487728 | solution.py:54
  507.9 0.6 copy-done.2
  508.5 2.5 compare_and_fusion
  511.0 0.1 copy.24
  511.1 12.5 %fusion.29 = (f32[2,128]{1,0:T(2,128)S(1)}, f32[2,128,16384]{2,1,0:T(8,128)}) fusion(bf16[128,2,128]{0,2,1:T(8,128)(2,1)S(1)} %bitcast.37, bf16[16384,2,128]{0,2,1:T(8,128)(2,1)} %get-tuple-element.78, pred[128,16384]{1,0:T(8,128)(4,1)S(1)} %compare_and_fusion), kind=kOutput, calls=%fused_computation.49 | convolution fusion | flops 1082130176 | bytes 27329536 | tf_op jit(solution)/shard_map/cond/branch_1_fun/qhd,khd->hqk/dot_general | solution.py:32
  523.6 10.5 %fusion.2 = f32[2,128,128]{1,2,0:T(8,128)S(1)} fusion(bf16[16384,2,128]{0,2,1:T(8,128)(2,1)} %get-tuple-element.79, f32[2,128,16384]{2,1,0:T(8,128)} %get-tuple-element.94, f32[2,128]{1,0:T(2,128)S(1)} %broadcast_maximum_fusion, pred[128,16384]{1,0:T(8,128)(4,1)S(1)} %compare_and_fusion), kind=kOutput, calls=%fused_computation.4 | convolution fusion | flops 1086324736 | bytes 27395072 | tf_op jit(solution)/shard_map/cond | solution.py:54
  534.1 8.0 %fusion.1 = f32[2,128]{1,0:T(2,128)S(1)} fusion(f32[2,128,16384]{2,1,0:T(8,128)} %get-tuple-element.94, f32[2,128]{1,0:T(2,128)S(1)} %broadcast_maximum_fusion, pred[128,16384]{1,0:T(8,128)(4,1)S(1)} %compare_and_fusion), kind=kLoop, calls=%fused_computation.3 | loop fusion | flops 12582656 | bytes 18876416 | tf_op jit(solution)/shard_map/cond/branch_1_fun/reduce_sum | solution.py:42
  542.2 33.9 %conditional.3 = (f32[2,128]{1,0:T(2,128)S(1)}, f32[2,128,128]{1,2,0:T(8,128)S(1)}) conditional(s32[]{:T(128)} %convert_element_type.68, () %tuple.23, (s32[16384]{0:T(1024)S(1)}, s32[128]{0:T(128)S(1)}, f32[16384]{0:T(1024)}, f32[128]{0:T(128)S(1)}, bf16[256,256]{1,0:T(8,128)(2,1)S(1)}, /*index=5*/bf16[16384,2,128]{0,2,1:T(8,128)(2,1)}, ...), branch_computations={%region_9.10_spmd, %region_10.13_spmd} | conditional | flops 2187329280 | bytes 76225552 | solution.py:54
  542.4 2.5 compare_and_fusion.1
  545.0 0.1 copy.28
  545.1 12.5 %fusion.30 = (f32[2,128]{1,0:T(2,128)S(1)}, f32[2,128,16384]{2,1,0:T(8,128)}) fusion(bf16[128,2,128]{0,2,1:T(8,128)(2,1)S(1)} %bitcast.38, bf16[16384,2,128]{0,2,1:T(8,128)(2,1)} %get-tuple-element.85, pred[128,16384]{1,0:T(8,128)(4,1)S(1)} %compare_and_fusion.1), kind=kOutput, calls=%fused_computation.50 | convolution fusion | flops 1082130176 | bytes 27329536 | tf_op jit(solution)/shard_map/cond/branch_1_fun/qhd,khd->hqk/dot_general | solution.py:32
  557.6 10.5 %fusion.10 = f32[2,128,128]{1,2,0:T(8,128)S(1)} fusion(bf16[16384,2,128]{0,2,1:T(8,128)(2,1)} %get-tuple-element.86, f32[2,128,16384]{2,1,0:T(8,128)} %get-tuple-element.96, f32[2,128]{1,0:T(2,128)S(1)} %broadcast_maximum_fusion.1, pred[128,16384]{1,0:T(8,128)(4,1)S(1)} %compare_and_fusion.1), kind=kOutput, calls=%fused_computation.15 | convolution fusion | flops 1086324736 | bytes 27395072 | tf_op jit(solution)/shard_map/cond | solution.py:54
  568.1 8.0 %fusion.9 = f32[2,128]{1,0:T(2,128)S(1)} fusion(f32[2,128,16384]{2,1,0:T(8,128)} %get-tuple-element.96, f32[2,128]{1,0:T(2,128)S(1)} %broadcast_maximum_fusion.1, pred[128,16384]{1,0:T(8,128)(4,1)S(1)} %compare_and_fusion.1), kind=kLoop, calls=%fused_computation.14 | loop fusion | flops 12582656 | bytes 18876416 | tf_op jit(solution)/shard_map/cond/branch_1_fun/reduce_sum | solution.py:42
  576.1 1.3 fusion.24
  577.5 25.1 %reduce-scatter.2.cloned.1.call-done = f32[256,256]{1,0:T(8,128)} async-done(((f32[256,1024]{1,0:T(8,128)}), f32[256,256]{1,0:T(8,128)}) %reduce-scatter.2.cloned.1.call-update) | async-done | bytes 262160 | tf_op jit(solution)/shard_map/reduce_scatter | solution.py:110
  602.6 1.6 convert_element_type.72
  (26 shorter events, 0.3 us)
Async XLA Ops:
  6.5 569.6 %copy-start = (bf16[256,1024]{1,0:T(8,128)(2,1)S(1)}, bf16[256,1024]{1,0:T(8,128)(2,1)}, u32[]{:S(2)}) copy-start(bf16[256,1024]{1,0:T(8,128)(2,1)} %param.12) | copy-start | bytes 1572868
  29.6 12.4 %copy-start.3 = (s32[256]{0:T(256)S(1)}, s32[256]{0:T(256)}, u32[]{:S(2)}) copy-start(s32[256]{0:T(256)} %param.13) | copy-start | bytes 3076
  29.6 416.7 %all-to-all-start = ((bf16[64,2,256,256]{2,3,1,0:T(8,128)(2,1)}), bf16[64,2,256,256]{2,3,1,0:T(8,128)(2,1)}, u32[]{:S(2)}, u32[]{:S(2)}) async-start(bf16[64,2,256,256]{2,3,1,0:T(8,128)(2,1)} %stack.11), calls=%async_computation | async-start | bytes 33554432 | tf_op jit(solution)/shard_map/all_to_all | solution.py:100
  41.9 560.7 %reduce-scatter.2.cloned.1.call-start = ((), (), s32[]{:S(2)}) async-start(), calls=%async_computation.2 | async-start | bytes 1310720 | tf_op jit(solution)/shard_map/reduce_scatter | solution.py:110
  440.3 67.3 %copy-start.1 = (f32[64,1,256]{2,1,0:T(1,128)}, f32[64,1,256]{2,1,0:T(1,128)S(1)}, u32[]{:S(2)}) copy-start(f32[64,1,256]{2,1,0:T(1,128)S(1)} %convert_element_type.74) | copy-start | bytes 196612
  507.8 0.6 copy-start.2
Sparse Core Ops, SparseCore 0:
  577.6 24.9 reduce-scatter.1
